TPU v7x, 256 devices: a whole 4x4x8 slice. The times are simulated.
256 devices in a mesh: dp: 8 (over y, x_hi), mp: 32 (over z, x_lo, core).
Axes of the slice: x: 4 (x_hi: 2, x_lo: 2; x = x_hi * 2 + x_lo), y: 4, z: 8, core: 2. Of those that a mesh axis runs over, the one named last changes fastest.
Arguments:
- activations: bfloat16 [4096, 4096], P('dp', 'mp'), may hold values from -22 to 22
- out_grads: bfloat16 [4096, 32768], P('dp', 'mp'), may hold values from -1 to 1
- weight: float32 [4096, 32768], P('dp', 'mp'), may hold values from -0.09375 to 0.09375
- row_state: float32 [4096], P('dp'), may hold values from 0.1 to 1.6
- column_state: float32 [32768], P('mp'), may hold values from 0.1 to 1.6
- next_batch: bfloat16 [4096, 4096], P('dp', 'mp'), may hold values from -6 to 6
Outputs:
- new_weight: float32 [4096, 32768], P('dp', 'mp')
- update: float32 [4096, 32768], P('dp', 'mp')
- row_moment: float32 [4096], P('dp')
- column_moment: float32 [32768], P('mp')
- next_hidden: bfloat16 [4096, 32768], P('dp', 'mp')
All inputs are finite; a program needn't handle non-finite values.
Results may differ from a plain program's by a relative error of at most 0.001.
The roundings to bfloat16 on the way count: a program that leaves them out, or rounds other values in their place, can miss the bound.
Values may be sent and summed in bfloat16 or wider, within the bound.
A program may use at most 128 MiB of HBM per device.

v0:
```python
import jax
import jax.numpy as jnp
from jax import lax
from jax.sharding import PartitionSpec as P

D = 4096
FF = 32768
tiny_square = 1e-30
weight_eps = 1e-06
decay_rate = 0.5
clip_level = 0.5
learn_rate = 0.01


def body(activations, out_grads, weight, row_state, column_state, next_batch):
    features, next_features = (
        lax.all_gather(activations, "mp", axis=1, tiled=True),
        lax.all_gather(next_batch, "mp", axis=1, tiled=True),
    )
    contract = (((0,), (0,)), ((), ()))
    block = features
    gradient = lax.psum_scatter(
        lax.dot_general(block, out_grads, contract, preferred_element_type=jnp.float32),
        "dp",
        scatter_dimension=0,
        tiled=True,
    )
    squares = gradient * gradient + tiny_square
    row_part = jnp.sum(squares, axis=1)
    column_part = jnp.sum(squares, axis=0)
    row_sum = lax.psum(row_part, "mp")
    column_sum = lax.psum(column_part, "dp")
    row_moment = decay_rate * row_state + (1.0 - decay_rate) * (row_sum / FF)
    column_moment = decay_rate * column_state + (1.0 - decay_rate) * (column_sum / D)
    raw_update = gradient * lax.rsqrt(row_moment[:, None] * column_moment[None, :])
    raw_total, weight_total = lax.psum(
        (jnp.sum(raw_update * raw_update), jnp.sum(weight * weight)), ("dp", "mp")
    )
    rms_update = jnp.sqrt(raw_total / (D * FF))
    update = raw_update / jnp.maximum(1.0, rms_update / clip_level)
    rms_weight = jnp.sqrt(weight_total / (D * FF) + weight_eps)
    new_weight = weight - learn_rate * rms_weight * update
    weight_half = new_weight.astype(jnp.bfloat16)
    block = next_features
    hidden_sum = jnp.dot(
        block,
        lax.all_gather(weight_half, "dp", axis=0, tiled=True),
        preferred_element_type=jnp.float32,
    )
    return (new_weight, update, row_moment, column_moment, hidden_sum.astype(jnp.bfloat16))


def solution(mesh):
    return jax.shard_map(
        body,
        mesh=mesh,
        in_specs=(P("dp", "mp"), P("dp", "mp"), P("dp", "mp"), P("dp"), P("mp"), P("dp", "mp")),
        out_specs=(P("dp", "mp"), P("dp", "mp"), P("dp"), P("mp"), P("dp", "mp")),
        check_vma=False,
    )
```

profile of v0, /device:TPU:1, one launch (start us, length us, event | category | flops | bytes accessed | tf_op | source)
XLA Modules:
  0.0 577.7 jit_solution(11072777842069617354)
XLA Ops:
  7.2 0.0 copy-start
  7.2 0.0 all-gather.4.cloned.1.call-start
  7.2 0.7 all-gather.4.cloned.1.call-update
  7.9 0.0 reduce-scatter.2.cloned.1.call-start
  8.0 78.1 %all-gather.4.cloned.1.call-done = bf16[512,4096]{1,0:T(8,128)(2,1)} async-done(((bf16[512,128]{1,0:T(8,128)(2,1)}), bf16[512,4096]{1,0:T(8,128)(2,1)}) %all-gather.4.cloned.1.call-update) | async-done | bytes 4194320 | tf_op jit(solution)/shard_map/all_gather | solution.py:17
  86.1 0.0 copy-done
  86.1 10.4 %fusion.6 = f32[4096,1024]{1,0:T(8,128)} fusion(bf16[512,4096]{1,0:T(8,128)(2,1)} %all-gather.4.cloned.1.call-done, bf16[512,1024]{1,0:T(8,128)(2,1)S(1)} %copy-done), kind=kOutput, calls=%fused_computation.13 | convolution fusion | flops 4294967296 | bytes 22020096 | tf_op jit(solution)/shard_map/dot_general | solution.py:23
  96.5 0.0 reduce-scatter.2.cloned.1.call-update
  96.5 0.0 all-gather.8.cloned.1.call-start
  96.5 0.7 all-gather.8.cloned.1.call-update
  97.2 0.0 copy-start.6
  97.3 0.0 copy-start.5
  97.3 0.0 all-gather.6.cloned.1.call-start
  97.3 0.8 copy-done.2
  98.1 1.1 multiply_reduce_fusion.1
  99.2 191.7 %reduce-scatter.2.cloned.1.call-done = f32[512,1024]{1,0:T(8,128)} async-done(((f32[4096,1024]{1,0:T(8,128)}), f32[512,1024]{1,0:T(8,128)}) %reduce-scatter.2.cloned.1.call-update) | async-done | bytes 2097168 | tf_op jit(solution)/shard_map/reduce_scatter | solution.py:22
  290.9 2.1 fusion.1
  293.1 56.9 %psum.29 = f32[512]{0:T(512)S(1)} all-reduce(f32[512]{0:T(512)S(1)} %get-tuple-element.10), channel_id=1, replica_groups=mesh['dp'=8,'mp'=32] {'mp'}, use_global_device_ids=true, to_apply=%region_4.0 | all-reduce | flops 512 | bytes 4096 | tf_op jit(solution)/shard_map/psum | solution.py:31
  350.0 18.5 %psum.30 = f32[1024]{0:T(1024)S(1)} all-reduce(f32[1024]{0:T(1024)S(1)} %get-tuple-element.11), channel_id=1, replica_groups=mesh['dp'=8,'mp'=32] {'dp'}, use_global_device_ids=true, to_apply=%region_6.0 | all-reduce | flops 1024 | bytes 8192 | tf_op jit(solution)/shard_map/psum | solution.py:32
  368.4 0.0 copy-done.6
  368.5 0.0 copy-done.5
  368.5 0.0 copy-start.4
  368.5 0.0 copy-done.1
  368.5 0.0 copy-start.3
  368.5 1.5 multiply_reduce_fusion
  370.0 76.3 %all-reduce = (f32[]{:T(128)}, f32[]{:T(128)}) all-reduce(f32[]{:T(128)} %multiply_reduce_fusion, f32[]{:T(128)} %multiply_reduce_fusion.1), channel_id=1, replica_groups=mesh['dp'=8,'mp'=32] {'dp','mp'}, use_global_device_ids=true, to_apply=%region_8.0 | all-reduce | flops 2 | bytes 16 | tf_op jit(solution)/shard_map/psum | solution.py:36
  447.7 4.5 fusion.4
  452.2 0.0 all-gather.6.cloned.1.call-update
  452.3 0.0 all-gather.8.cloned.1.call-done
  452.3 108.4 %all-gather.6.cloned.1.call-done = bf16[4096,1024]{1,0:T(8,128)(2,1)} async-done(((bf16[512,1024]{1,0:T(8,128)(2,1)}), bf16[4096,1024]{1,0:T(8,128)(2,1)}) %all-gather.6.cloned.1.call-update) | async-done | bytes 8388624 | tf_op jit(solution)/shard_map/all_gather | solution.py:47
  560.7 9.1 %fusion.3 = bf16[512,1024]{0,1:T(8,128)(2,1)S(1)} fusion(bf16[4096,1024]{1,0:T(8,128)(2,1)} %all-gather.6.cloned.1.call-done, bf16[512,4096]{1,0:T(8,128)(2,1)} %all-gather.8.cloned.1.call-done), kind=kOutput, calls=%fused_computation.9 | convolution fusion | flops 4295491584 | bytes 13631488 | tf_op jit(solution)/shard_map/dot_general | solution.py:45
  569.8 1.3 copy.11
  (6 shorter events, 0.0 us)
Async XLA Ops:
  7.2 78.9 %copy-start = (bf16[512,1024]{1,0:T(8,128)(2,1)S(1)}, bf16[512,1024]{1,0:T(8,128)(2,1)}, u32[]{:S(2)}) copy-start(bf16[512,1024]{1,0:T(8,128)(2,1)} %param.7) | copy-start | bytes 3145732
  7.2 78.9 %all-gather.4.cloned.1.call-start = ((), (), s32[]{:S(2)}) async-start(), calls=%async_computation.1 | async-start | bytes 4325376 | tf_op jit(solution)/shard_map/all_gather | solution.py:17
  7.9 283.0 %reduce-scatter.2.cloned.1.call-start = ((), (), s32[]{:S(2)}) async-start(), calls=%async_computation.2 | async-start | bytes 18874368 | tf_op jit(solution)/shard_map/reduce_scatter | solution.py:22
  96.5 1.6 copy-start.2
  96.5 355.8 %all-gather.8.cloned.1.call-start = ((), (), s32[]{:S(2)}) async-start(), calls=%async_computation.4 | async-start | bytes 4325376 | tf_op jit(solution)/shard_map/all_gather | solution.py:18
  97.2 271.2 %copy-start.6 = (f32[512]{0:T(512)S(1)}, f32[512]{0:T(512)}, u32[]{:S(2)}) copy-start(f32[512]{0:T(512)} %param.9) | copy-start | bytes 6148
  97.3 271.2 %copy-start.5 = (f32[1024]{0:T(1024)S(1)}, f32[1024]{0:T(1024)}, u32[]{:S(2)}) copy-start(f32[1024]{0:T(1024)} %param.10) | copy-start | bytes 12292
  97.3 463.4 %all-gather.6.cloned.1.call-start = ((), (), s32[]{:S(2)}) async-start(), calls=%async_computation.3 | async-start | bytes 9437184 | tf_op jit(solution)/shard_map/all_gather | solution.py:47
  290.9 77.6 %copy-start.1 = (f32[512,1024]{1,0:T(8,128)S(1)}, f32[512,1024]{1,0:T(8,128)}, u32[]{:S(2)}) copy-start(f32[512,1024]{1,0:T(8,128)} %reduce-scatter.2.cloned.1.call-done) | copy-start | bytes 6291460
  368.5 83.8 %copy-start.4 = (f32[512]{0:T(512)}, f32[512]{0:T(512)S(1)}, u32[]{:S(2)}) copy-start(f32[512]{0:T(512)S(1)} %multiply_add_fusion.2) | copy-start | bytes 6148
  368.5 83.7 %copy-start.3 = (f32[1024]{0:T(1024)}, f32[1024]{0:T(1024)S(1)}, u32[]{:S(2)}) copy-start(f32[1024]{0:T(1024)S(1)} %multiply_add_fusion.1) | copy-start | bytes 12292
Sparse Core Ops, SparseCore 0:
  9.8 76.3 all-gather.3
  96.6 194.2 reduce-scatter.1
  292.7 75.3 all-gather.7
  452.4 108.2 all-gather.5
where the time goes:
time: 578 us
  waiting for transfers between devices  380 us (66%)
  blocking collectives  152 us (26%)
  matrix products  19.5 us (3%)
  between operations  15.2 us (3%)
  other arithmetic  9.27 us (2%)
    reduce_scatter x1, waiting for transfers between devices, body(): lax.psum_scatter(lax.dot_general(block, out_grads, contract, preferred_el...  192 us
    all_gather x1, waiting for transfers between devices, body(): lax.all_gather(weight_half, 'dp', axis=0, tiled=True)  108 us
    all_gather x1, waiting for transfers between devices, body(): lax.all_gather(activations, 'mp', axis=1, tiled=True)  78.1 us
    psum x1, blocking collectives, body(): lax.psum((jnp.sum(raw_update * raw_update), jnp.sum(weight * weight)), ('...  76.3 us
    psum x1, blocking collectives, body(): row_sum = lax.psum(row_part, 'mp')  56.9 us
    psum x1, blocking collectives, body(): column_sum = lax.psum(column_part, 'dp')  18.5 us
  transfers between devices with their start and end apart: 4, of which 3 were waited for; matrix products, arithmetic and copies ran while one was open for 2% of the time, Pallas kernels for 0%

commit v1 on v0

--- a/solution.py
+++ b/solution.py
@@ -14,7 +14,9 @@
 
 def body(activations, out_grads, weight, row_state, column_state, next_batch):
     features, next_features = (
-        lax.all_gather(activations, "mp", axis=1, tiled=True),
+        jnp.concatenate(
+            lax.all_to_all(jnp.stack([activations] * lax.axis_size("mp")), "mp", 0, 0), axis=1
+        ),
         lax.all_gather(next_batch, "mp", axis=1, tiled=True),
     )
     contract = (((0,), (0,)), ((), ()))

time: 578 us -> 617 us (1.067)
  blocking collectives: 152 us -> 257 us
  waiting for transfers between devices: 380 us -> 312 us
    all_to_all x0 -> x1, blocking collectives: none -> 106 us  [body(): lax.all_to_all(jnp.stack([activations] * lax.axis_size('mp')), 'mp', 0, 0)]
    all_gather x1 -> x0, waiting for transfers between devices: 78.1 us -> none  [body(): lax.all_gather(activations, 'mp', axis=1, tiled=True)]
    reduce_scatter x1, waiting for transfers between devices: 192 us -> 203 us  [body(): lax.psum_scatter(lax.dot_general(block, out_grads, contract, preferred_el...]
  transfers between devices with their start and end apart: 4 -> 3, of which waited for: 3 -> 2; matrix products, arithmetic and copies ran while one was open for 2% -> 2% of each run, Pallas kernels for 0% -> 0%
where the time goes in v1:
time: 617 us
  waiting for transfers between devices  312 us (51%)
  blocking collectives  257 us (42%)
  matrix products  17.2 us (3%)
  between operations  17 us (3%)
  other arithmetic  9.27 us (2%)
    reduce_scatter x1, waiting for transfers between devices, body(): lax.psum_scatter(lax.dot_general(block, out_grads, contract, preferred_el...  203 us
    all_gather x1, waiting for transfers between devices, body(): lax.all_gather(weight_half, 'dp', axis=0, tiled=True)  109 us
    all_to_all x1, blocking collectives, body(): lax.all_to_all(jnp.stack([activations] * lax.axis_size('mp')), 'mp', 0, 0)  106 us
    psum x1, blocking collectives, body(): lax.psum((jnp.sum(raw_update * raw_update), jnp.sum(weight * weight)), ('...  76.1 us
    psum x1, blocking collectives, body(): row_sum = lax.psum(row_part, 'mp')  56.4 us
    psum x1, blocking collectives, body(): column_sum = lax.psum(column_part, 'dp')  18.5 us
  transfers between devices with their start and end apart: 3, of which 2 were waited for; matrix products, arithmetic and copies ran while one was open for 2% of the time, Pallas kernels for 0%

profile of v1, /device:TPU:1, one launch (start us, length us, event | category | flops | bytes accessed | tf_op | source)
XLA Modules:
  0.0 616.8 jit_solution(18198121364845942252)
XLA Ops:
  8.0 0.0 copy-start
  8.0 0.0 reduce-scatter.2.cloned.1.call-start
  8.1 1.1 copy.12
  9.1 0.5 stack.2
  9.6 106.3 %all_to_all.5 = bf16[32,512,128]{1,2,0:T(8,128)(2,1)S(1)} all-to-all(bf16[32,512,128]{1,2,0:T(8,128)(2,1)S(1)} %stack.2), channel_id=1, replica_groups=mesh['dp'=8,'mp'=32] {'mp'}, dimensions={0} | all-to-all | bytes 8388608 | tf_op jit(solution)/shard_map/all_to_all | solution.py:18
  115.9 0.0 copy-done
  115.9 8.1 %fusion.6 = f32[4096,1024]{1,0:T(8,128)} fusion(bf16[512,4096]{0,1:T(8,128)(2,1)S(1)} %bitcast.9, bf16[512,1024]{1,0:T(8,128)(2,1)S(1)} %copy-done), kind=kOutput, calls=%fused_computation.13 | convolution fusion | flops 4294967296 | bytes 22020096 | tf_op jit(solution)/shard_map/dot_general | solution.py:25
  124.0 0.0 reduce-scatter.2.cloned.1.call-update
  124.0 0.0 all-gather.5.cloned.1.call-start
  124.1 0.5 all-gather.5.cloned.1.call-update
  124.6 0.0 copy-start.6
  124.6 0.0 copy-start.5
  124.6 0.0 all-gather.3.cloned.1.call-start
  124.7 0.9 copy-done.2
  125.6 1.1 multiply_reduce_fusion.1
  126.7 202.8 %reduce-scatter.2.cloned.1.call-done = f32[512,1024]{1,0:T(8,128)} async-done(((f32[4096,1024]{1,0:T(8,128)}), f32[512,1024]{1,0:T(8,128)}) %reduce-scatter.2.cloned.1.call-update) | async-done | bytes 2097168 | tf_op jit(solution)/shard_map/reduce_scatter | solution.py:24
  329.5 2.1 fusion.1
  331.7 56.4 %psum.29 = f32[512]{0:T(512)S(1)} all-reduce(f32[512]{0:T(512)S(1)} %get-tuple-element.15), channel_id=1, replica_groups=mesh['dp'=8,'mp'=32] {'mp'}, use_global_device_ids=true, to_apply=%region_4.0 | all-reduce | flops 512 | bytes 4096 | tf_op jit(solution)/shard_map/psum | solution.py:33
  388.1 18.5 %psum.30 = f32[1024]{0:T(1024)S(1)} all-reduce(f32[1024]{0:T(1024)S(1)} %get-tuple-element.16), channel_id=1, replica_groups=mesh['dp'=8,'mp'=32] {'dp'}, use_global_device_ids=true, to_apply=%region_6.0 | all-reduce | flops 1024 | bytes 8192 | tf_op jit(solution)/shard_map/psum | solution.py:34
  406.5 0.0 copy-done.6
  406.6 0.0 copy-done.5
  406.6 0.0 copy-start.4
  406.6 0.0 copy-done.1
  406.6 0.0 copy-start.3
  406.6 1.5 multiply_reduce_fusion
  408.1 76.1 %all-reduce = (f32[]{:T(128)}, f32[]{:T(128)}) all-reduce(f32[]{:T(128)} %multiply_reduce_fusion, f32[]{:T(128)} %multiply_reduce_fusion.1), channel_id=1, replica_groups=mesh['dp'=8,'mp'=32] {'dp','mp'}, use_global_device_ids=true, to_apply=%region_8.0 | all-reduce | flops 2 | bytes 16 | tf_op jit(solution)/shard_map/psum | solution.py:38
  485.6 4.5 fusion.4
  490.1 0.0 all-gather.3.cloned.1.call-update
  490.1 0.0 all-gather.5.cloned.1.call-done
  490.2 108.8 %all-gather.3.cloned.1.call-done = bf16[4096,1024]{1,0:T(8,128)(2,1)} async-done(((bf16[512,1024]{1,0:T(8,128)(2,1)}), bf16[4096,1024]{1,0:T(8,128)(2,1)}) %all-gather.3.cloned.1.call-update) | async-done | bytes 8388624 | tf_op jit(solution)/shard_map/all_gather | solution.py:49
  599.0 9.1 %fusion.3 = bf16[512,1024]{0,1:T(8,128)(2,1)S(1)} fusion(bf16[4096,1024]{1,0:T(8,128)(2,1)} %all-gather.3.cloned.1.call-done, bf16[512,4096]{1,0:T(8,128)(2,1)} %all-gather.5.cloned.1.call-done), kind=kOutput, calls=%fused_computation.9 | convolution fusion | flops 4295491584 | bytes 13631488 | tf_op jit(solution)/shard_map/dot_general | solution.py:47
  608.1 1.3 copy.13
  (6 shorter events, 0.0 us)
Async XLA Ops:
  8.0 107.9 %copy-start = (bf16[512,1024]{1,0:T(8,128)(2,1)S(1)}, bf16[512,1024]{1,0:T(8,128)(2,1)}, u32[]{:S(2)}) copy-start(bf16[512,1024]{1,0:T(8,128)(2,1)} %param.7) | copy-start | bytes 3145732
  8.0 321.5 %reduce-scatter.2.cloned.1.call-start = ((), (), s32[]{:S(2)}) async-start(), calls=%async_computation.2 | async-start | bytes 18874368 | tf_op jit(solution)/shard_map/reduce_scatter | solution.py:24
  124.0 1.6 copy-start.2
  124.0 366.1 %all-gather.5.cloned.1.call-start = ((), (), s32[]{:S(2)}) async-start(), calls=%async_computation.4 | async-start | bytes 4325376 | tf_op jit(solution)/shard_map/all_gather | solution.py:20
  124.6 282.0 %copy-start.6 = (f32[512]{0:T(512)S(1)}, f32[512]{0:T(512)}, u32[]{:S(2)}) copy-start(f32[512]{0:T(512)} %param.9) | copy-start | bytes 6148
  124.6 282.0 %copy-start.5 = (f32[1024]{0:T(1024)S(1)}, f32[1024]{0:T(1024)}, u32[]{:S(2)}) copy-start(f32[1024]{0:T(1024)} %param.10) | copy-start | bytes 12292
  124.6 474.4 %all-gather.3.cloned.1.call-start = ((), (), s32[]{:S(2)}) async-start(), calls=%async_computation.3 | async-start | bytes 9437184 | tf_op jit(solution)/shard_map/all_gather | solution.py:49
  329.5 77.1 %copy-start.1 = (f32[512,1024]{1,0:T(8,128)S(1)}, f32[512,1024]{1,0:T(8,128)}, u32[]{:S(2)}) copy-start(f32[512,1024]{1,0:T(8,128)} %reduce-scatter.2.cloned.1.call-done) | copy-start | bytes 6291460
  406.6 83.5 %copy-start.4 = (f32[512]{0:T(512)}, f32[512]{0:T(512)S(1)}, u32[]{:S(2)}) copy-start(f32[512]{0:T(512)S(1)} %multiply_add_fusion.2) | copy-start | bytes 6148
  406.6 83.5 %copy-start.3 = (f32[1024]{0:T(1024)}, f32[1024]{0:T(1024)S(1)}, u32[]{:S(2)}) copy-start(f32[1024]{0:T(1024)S(1)} %multiply_add_fusion.1) | copy-start | bytes 12292
Sparse Core Ops, SparseCore 0:
  124.1 205.3 reduce-scatter.1
Sparse Core Ops, SparseCore 1:
  126.3 83.1 all-gather.4
  490.2 108.7 all-gather.2

commit v2 on v0

--- a/solution.py
+++ b/solution.py
@@ -28,7 +28,7 @@
     squares = gradient * gradient + tiny_square
     row_part = jnp.sum(squares, axis=1)
     column_part = jnp.sum(squares, axis=0)
-    row_sum = lax.psum(row_part, "mp")
+    row_sum = jnp.sum(lax.all_gather(row_part, "mp"), axis=0)
     column_sum = lax.psum(column_part, "dp")
     row_moment = decay_rate * row_state + (1.0 - decay_rate) * (row_sum / FF)
     column_moment = decay_rate * column_state + (1.0 - decay_rate) * (column_sum / D)

time: 578 us -> 557 us (0.964)
  blocking collectives: 152 us -> 131 us
    psum x1 -> x0, blocking collectives: 56.9 us -> none  [body(): row_sum = lax.psum(row_part, 'mp')]
    all_gather x0 -> x1, blocking collectives: none -> 38.2 us  [body(): row_sum = jnp.sum(lax.all_gather(row_part, 'mp'), axis=0)]
where the time goes in v2:
time: 557 us
  waiting for transfers between devices  379 us (68%)
  blocking collectives  131 us (24%)
  matrix products  19.5 us (4%)
  between operations  15.2 us (3%)
  other arithmetic  9.33 us (2%)
    reduce_scatter x1, waiting for transfers between devices, body(): lax.psum_scatter(lax.dot_general(block, out_grads, contract, preferred_el...  192 us
    all_gather x1, waiting for transfers between devices, body(): lax.all_gather(weight_half, 'dp', axis=0, tiled=True)  108 us
    all_gather x1, waiting for transfers between devices, body(): lax.all_gather(activations, 'mp', axis=1, tiled=True)  78.1 us
    psum x1, blocking collectives, body(): lax.psum((jnp.sum(raw_update * raw_update), jnp.sum(weight * weight)), ('...  74.3 us
    all_gather x1, blocking collectives, body(): row_sum = jnp.sum(lax.all_gather(row_part, 'mp'), axis=0)  38.2 us
    psum x1, blocking collectives, body(): column_sum = lax.psum(column_part, 'dp')  18.6 us
  transfers between devices with their start and end apart: 4, of which 3 were waited for; matrix products, arithmetic and copies ran while one was open for 2% of the time, Pallas kernels for 0%

profile of v2, /device:TPU:1, one launch (start us, length us, event | category | flops | bytes accessed | tf_op | source)
XLA Modules:
  0.0 556.8 jit_solution(1035655176002972448)
XLA Ops:
  7.2 0.0 copy-start
  7.2 0.0 all-gather.6.cloned.1.call-start
  7.2 0.7 all-gather.6.cloned.1.call-update
  7.9 0.0 reduce-scatter.2.cloned.1.call-start
  8.0 78.1 %all-gather.6.cloned.1.call-done = bf16[512,4096]{1,0:T(8,128)(2,1)} async-done(((bf16[512,128]{1,0:T(8,128)(2,1)}), bf16[512,4096]{1,0:T(8,128)(2,1)}) %all-gather.6.cloned.1.call-update) | async-done | bytes 4194320 | tf_op jit(solution)/shard_map/all_gather | solution.py:17
  86.1 0.0 copy-done
  86.1 10.4 %fusion.6 = f32[4096,1024]{1,0:T(8,128)} fusion(bf16[512,4096]{1,0:T(8,128)(2,1)} %all-gather.6.cloned.1.call-done, bf16[512,1024]{1,0:T(8,128)(2,1)S(1)} %copy-done), kind=kOutput, calls=%fused_computation.13 | convolution fusion | flops 4294967296 | bytes 22020096 | tf_op jit(solution)/shard_map/dot_general | solution.py:23
  96.5 0.0 reduce-scatter.2.cloned.1.call-update
  96.5 0.0 all-gather.10.cloned.1.call-start
  96.5 0.7 all-gather.10.cloned.1.call-update
  97.2 0.0 copy-start.6
  97.3 0.0 copy-start.5
  97.3 0.0 all-gather.8.cloned.1.call-start
  97.3 0.8 copy-done.2
  98.1 1.1 multiply_reduce_fusion.1
  99.2 191.7 %reduce-scatter.2.cloned.1.call-done = f32[512,1024]{1,0:T(8,128)} async-done(((f32[4096,1024]{1,0:T(8,128)}), f32[512,1024]{1,0:T(8,128)}) %reduce-scatter.2.cloned.1.call-update) | async-done | bytes 2097168 | tf_op jit(solution)/shard_map/reduce_scatter | solution.py:22
  290.9 2.1 fusion.1
  293.1 38.2 %all-gather.1 = f32[32,1,512]{2,1,0:T(1,128)S(1)} all-gather(f32[1,1,512]{2,1,0:T(1,128)S(1)} %bitcast.7), channel_id=2, replica_groups=mesh['dp'=8,'mp'=32] {'mp'}, dimensions={0}, use_global_device_ids=true | all-gather | bytes 67584 | tf_op jit(solution)/shard_map/all_gather | solution.py:31
  331.3 0.1 reduce_sum.47
  331.4 18.6 %psum.22 = f32[1024]{0:T(1024)S(1)} all-reduce(f32[1024]{0:T(1024)S(1)} %get-tuple-element.16), channel_id=1, replica_groups=mesh['dp'=8,'mp'=32] {'dp'}, use_global_device_ids=true, to_apply=%region_6.0 | all-reduce | flops 1024 | bytes 8192 | tf_op jit(solution)/shard_map/psum | solution.py:32
  350.0 0.0 copy-done.6
  350.0 0.0 copy-done.5
  350.0 0.0 copy-start.4
  350.1 0.0 copy-start.3
  350.1 1.5 multiply_reduce_fusion
  351.6 74.3 %all-reduce = (f32[]{:T(128)}, f32[]{:T(128)}) all-reduce(f32[]{:T(128)} %multiply_reduce_fusion, f32[]{:T(128)} %multiply_reduce_fusion.1), channel_id=1, replica_groups=mesh['dp'=8,'mp'=32] {'dp','mp'}, use_global_device_ids=true, to_apply=%region_8.0 | all-reduce | flops 2 | bytes 16 | tf_op jit(solution)/shard_map/psum | solution.py:36
  427.3 4.5 fusion.4
  431.8 0.0 all-gather.8.cloned.1.call-update
  431.8 0.0 all-gather.10.cloned.1.call-done
  431.8 108.0 %all-gather.8.cloned.1.call-done = bf16[4096,1024]{1,0:T(8,128)(2,1)} async-done(((bf16[512,1024]{1,0:T(8,128)(2,1)}), bf16[4096,1024]{1,0:T(8,128)(2,1)}) %all-gather.8.cloned.1.call-update) | async-done | bytes 8388624 | tf_op jit(solution)/shard_map/all_gather | solution.py:47
  539.8 9.1 %fusion.3 = bf16[512,1024]{0,1:T(8,128)(2,1)S(1)} fusion(bf16[4096,1024]{1,0:T(8,128)(2,1)} %all-gather.8.cloned.1.call-done, bf16[512,4096]{1,0:T(8,128)(2,1)} %all-gather.10.cloned.1.call-done), kind=kOutput, calls=%fused_computation.9 | convolution fusion | flops 4295491584 | bytes 13631488 | tf_op jit(solution)/shard_map/dot_general | solution.py:45
  548.9 1.3 copy.12
  (7 shorter events, 0.0 us)
Async XLA Ops:
  7.2 78.9 %copy-start = (bf16[512,1024]{1,0:T(8,128)(2,1)S(1)}, bf16[512,1024]{1,0:T(8,128)(2,1)}, u32[]{:S(2)}) copy-start(bf16[512,1024]{1,0:T(8,128)(2,1)} %param.7) | copy-start | bytes 3145732
  7.2 78.9 %all-gather.6.cloned.1.call-start = ((), (), s32[]{:S(2)}) async-start(), calls=%async_computation.1 | async-start | bytes 4325376 | tf_op jit(solution)/shard_map/all_gather | solution.py:17
  7.9 283.0 %reduce-scatter.2.cloned.1.call-start = ((), (), s32[]{:S(2)}) async-start(), calls=%async_computation.2 | async-start | bytes 18874368 | tf_op jit(solution)/shard_map/reduce_scatter | solution.py:22
  96.5 1.6 copy-start.2
  96.5 335.3 %all-gather.10.cloned.1.call-start = ((), (), s32[]{:S(2)}) async-start(), calls=%async_computation.4 | async-start | bytes 4325376 | tf_op jit(solution)/shard_map/all_gather | solution.py:18
  97.2 252.8 %copy-start.6 = (f32[512]{0:T(512)S(1)}, f32[512]{0:T(512)}, u32[]{:S(2)}) copy-start(f32[512]{0:T(512)} %param.9) | copy-start | bytes 6148
  97.3 252.8 %copy-start.5 = (f32[1024]{0:T(1024)S(1)}, f32[1024]{0:T(1024)}, u32[]{:S(2)}) copy-start(f32[1024]{0:T(1024)} %param.10) | copy-start | bytes 12292
  97.3 442.5 %all-gather.8.cloned.1.call-start = ((), (), s32[]{:S(2)}) async-start(), calls=%async_computation.3 | async-start | bytes 9437184 | tf_op jit(solution)/shard_map/all_gather | solution.py:47
  290.9 59.2 %copy-start.1 = (f32[512,1024]{1,0:T(8,128)S(1)}, f32[512,1024]{1,0:T(8,128)}, u32[]{:S(2)}) copy-start(f32[512,1024]{1,0:T(8,128)} %reduce-scatter.2.cloned.1.call-done) | copy-start | bytes 6291460
  350.0 81.7 %copy-start.4 = (f32[512]{0:T(512)}, f32[512]{0:T(512)S(1)}, u32[]{:S(2)}) copy-start(f32[512]{0:T(512)S(1)} %multiply_add_fusion.2) | copy-start | bytes 6148
  350.1 81.7 %copy-start.3 = (f32[1024]{0:T(1024)}, f32[1024]{0:T(1024)S(1)}, u32[]{:S(2)}) copy-start(f32[1024]{0:T(1024)S(1)} %multiply_add_fusion.1) | copy-start | bytes 12292
Sparse Core Ops, SparseCore 0:
  9.8 76.3 all-gather.5
  96.6 194.2 reduce-scatter.1
  292.7 75.2 all-gather.9
  431.9 107.8 all-gather.7
